TPU v7x, 32 devices: a whole 2x2x4 slice. The times are simulated.
32 devices in a mesh: dp: 8 (over y, x, core), mp: 4 (over z).
Axes of the slice: x: 2, y: 2, z: 4, core: 2. Of those that a mesh axis runs over, the one named last changes fastest.
Arguments:
- token_block: int32 [8192, 1], P(('dp', 'mp')), may hold values from 0 to 31; in each aligned block of 256 rows (0 to 255, 256 to 511, ...) at most 16 rows name the same one
- token_offset: int32 [8192], P(('dp', 'mp')), may hold values from 0 to 15663
- lengths: int32 [128], P(('dp', 'mp')), may hold values from 1 to 64, as said below
- group_counts: int32 [109], replicated, may hold values from 1 to 16, 128 in all
- table: bfloat16 [501248, 768], P(('dp', 'mp')), may hold values from -6 to 6
- weight_qkv: bfloat16 [768, 2304], P(None, 'mp'), may hold values from -0.21875 to 0.21875
- bias_query: bfloat16 [768], P('mp'), may hold values from -2 to 2
- bias_value: bfloat16 [768], P('mp'), may hold values from -2 to 2
- weight_out: bfloat16 [768, 768], P('mp'), may hold values from -0.875 to 0.875
- bias_out: bfloat16 [768], replicated, may hold values from -2 to 2
- gain_one: bfloat16 [768], replicated, may hold values from 0.5 to 1.5
- shift_one: bfloat16 [768], replicated, may hold values from -2 to 2
- weight_in: bfloat16 [768, 3072], P(None, 'mp'), may hold values from -0.21875 to 0.21875
- bias_in: bfloat16 [3072], P('mp'), may hold values from -2 to 2
- weight_down: bfloat16 [3072, 768], P('mp'), may hold values from -0.15625 to 0.15625
- bias_down: bfloat16 [768], replicated, may hold values from -2 to 2
- gain_two: bfloat16 [768], replicated, may hold values from 0.5 to 1.5
- shift_two: bfloat16 [768], replicated, may hold values from -2 to 2
- cotangent: bfloat16 [8192, 768], P(('dp', 'mp')), may hold values from -6 to 6
Outputs:
- activations: bfloat16 [8192, 768], P(('dp', 'mp'))
- grad_table: float32 [501248, 768], P(('dp', 'mp'))
- grad_weight_qkv: float32 [768, 2304], P(None, 'mp')
- grad_bias_query: float32 [768], P('mp')
- grad_bias_value: float32 [768], P('mp')
- grad_weight_out: float32 [768, 768], P('mp')
- grad_bias_out: float32 [768], replicated
- grad_gain_one: float32 [768], replicated
- grad_shift_one: float32 [768], replicated
- grad_weight_in: float32 [768, 3072], P(None, 'mp')
- grad_bias_in: float32 [3072], P('mp')
- grad_weight_down: float32 [3072, 768], P('mp')
- grad_bias_down: float32 [768], replicated
- grad_gain_two: float32 [768], replicated
- grad_shift_two: float32 [768], replicated
Inputs may be any that keep to these rules, and one draw needn't show every extreme that they name: `token_block`: among the rows of one device, at most 16 tokens name the same block. `lengths`: positions from a sentence's length on are padding. `group_counts`: the counts sum to 128.
All inputs are finite; a program needn't handle non-finite values.
Results may differ from a plain program's by a relative error of at most 0.02.
Values may be sent and summed in bfloat16 or wider, within the bound.
A program may use at most 192 MiB of HBM per device.

v0:
```python
from functools import partial
import jax
import jax.numpy as jnp
from jax import lax
from jax.sharding import PartitionSpec as P

HD = 64
SEQ = 64
eps_norm = 1e-12


def norm_rows(hidden, gain_vec, shift_vec):
    row_mean = jnp.mean(hidden, axis=-1, keepdims=True)
    centred = hidden - row_mean
    variance = jnp.mean(centred * centred, axis=-1, keepdims=True)
    row_scale = lax.rsqrt(variance + eps_norm)
    normed = centred * row_scale
    return (normed * gain_vec + shift_vec, normed, row_scale)


def norm_back(grad_out, normed, row_scale, gain_vec):
    grad_normed = grad_out * gain_vec
    inner_mean = jnp.mean(grad_normed, axis=-1, keepdims=True)
    cross_mean = jnp.mean(grad_normed * normed, axis=-1, keepdims=True)
    grad_in = row_scale * (grad_normed - inner_mean - normed * cross_mean)
    return (grad_in, jnp.sum(grad_out * normed, axis=0), jnp.sum(grad_out, axis=0))


def on_device(
    token_block,
    token_offset,
    lengths,
    group_counts,
    table,
    weight_qkv,
    bias_query,
    bias_value,
    weight_out,
    bias_out,
    gain_one,
    shift_one,
    weight_in,
    bias_in,
    weight_down,
    bias_down,
    gain_two,
    shift_two,
    cotangent,
):
    f32 = jnp.float32
    bf16 = jnp.bfloat16
    devices = lax.axis_size(("dp", "mp"))
    tok_rows = token_offset.shape[0]
    model_width = table.shape[1]
    capacity = max(2, 2 * tok_rows // devices)
    token_owner = token_block[:, 0]
    owner_hits = (token_owner[:, None] == jnp.arange(devices, dtype=jnp.int32)[None, :]).astype(
        jnp.int32
    )
    slot_index = jnp.sum((jnp.cumsum(owner_hits, axis=0) - 1) * owner_hits, axis=1)
    slot_place = token_owner * capacity + slot_index
    requests = jnp.full((devices * capacity,), -1, jnp.int32).at[slot_place].set(token_offset)
    wanted = lax.all_to_all(
        requests.reshape(devices, capacity), ("dp", "mp"), split_axis=0, concat_axis=0, tiled=True
    )
    slot_live = wanted >= 0
    wanted_rows = jnp.maximum(wanted, 0)
    fetched = lax.all_to_all(
        table[wanted_rows], ("dp", "mp"), split_axis=0, concat_axis=0, tiled=True
    )
    embedded = fetched.reshape(devices * capacity, model_width)[slot_place]
    sent_local = lengths.shape[0]
    total_sent = sent_local * devices
    group_num = group_counts.shape[0]
    sent_index = lax.axis_index(("dp", "mp")) * sent_local + jnp.arange(sent_local, dtype=jnp.int32)
    offsets = jnp.cumsum(group_counts) - group_counts
    member = (sent_index[:, None] >= offsets[None, :]) & (
        sent_index[:, None] < (offsets + group_counts)[None, :]
    )
    group_weight = total_sent / (group_num * group_counts.astype(f32))
    sent_weight = jnp.sum(jnp.where(member, group_weight[None, :], f32(0.0)), axis=1)
    positions = jnp.arange(SEQ, dtype=f32)
    token_live = (positions[None, :] < lengths[:, None].astype(f32)).astype(f32)
    row_weight = (token_live * sent_weight[:, None]).reshape(tok_rows)
    count_local = jnp.sum(lengths).astype(f32)
    whole_in, whole_len = (
        lax.all_gather(embedded, "mp", axis=0, tiled=True),
        lax.all_gather(lengths.astype(bf16), "mp", axis=0, tiled=True),
    )
    rows_all = whole_in.shape[0]
    sentences_all = whole_len.shape[0]
    head_count = weight_qkv.shape[1] // (3 * HD)
    block_sent = min(8, sentences_all)
    block_count = sentences_all // block_sent
    mixed_qkv = jnp.dot(whole_in, weight_qkv, preferred_element_type=f32).reshape(
        rows_all, head_count, 3, HD
    )
    block_shape = (block_count, block_sent, SEQ, head_count, HD)
    queries = (
        (mixed_qkv[:, :, 0, :] + bias_query.astype(f32).reshape(head_count, HD))
        .astype(bf16)
        .reshape(block_shape)
    )
    key_rows = mixed_qkv[:, :, 1, :].astype(bf16).reshape(block_shape)
    value_rows = (
        (mixed_qkv[:, :, 2, :] + bias_value.astype(f32).reshape(head_count, HD))
        .astype(bf16)
        .reshape(block_shape)
    )
    len_blocks = whole_len.astype(f32).reshape(block_count, block_sent)

    def block_scores(q_blk, k_blk, len_blk):
        scores = jnp.einsum("sqhe,skhe->shqk", q_blk, k_blk, preferred_element_type=f32) * 0.125
        key_valid = positions[None, :] < len_blk[:, None]
        return jnp.where(key_valid[:, None, None, :], scores, f32(-1e30))

    def attend(block_items):
        q_blk, k_blk, v_blk, len_blk = block_items
        scores = block_scores(q_blk, k_blk, len_blk)
        row_max = jnp.max(scores, axis=-1, keepdims=True)
        exp_total = jnp.sum(jnp.exp(scores - row_max), axis=-1, keepdims=True)
        log_total = row_max + jnp.log(exp_total)
        attn_probs = jnp.exp(scores - log_total)
        context_blk = jnp.einsum(
            "shqk,skhe->sqhe", attn_probs.astype(bf16), v_blk, preferred_element_type=f32
        ).astype(bf16)
        return (context_blk, log_total[..., 0])

    context_blocks, log_totals = lax.map(attend, (queries, key_rows, value_rows, len_blocks))
    context = context_blocks.reshape(rows_all, head_count * HD)
    attn_sum = lax.psum_scatter(
        jnp.dot(context, weight_out, preferred_element_type=f32),
        "mp",
        scatter_dimension=0,
        tiled=True,
    )
    gain_one_f = gain_one.astype(f32)
    gain_two_f = gain_two.astype(f32)
    first_out, normed_one, scale_one = norm_rows(
        embedded.astype(f32) + attn_sum + bias_out.astype(f32), gain_one_f, shift_one.astype(f32)
    )
    whole_first = lax.all_gather(first_out.astype(bf16), "mp", axis=0, tiled=True)
    hidden_pre = jnp.dot(whole_first, weight_in, preferred_element_type=f32) + bias_in.astype(f32)
    gelu_val, gelu_pull = jax.vjp(partial(jax.nn.gelu, approximate=False), hidden_pre)
    hidden_act = gelu_val.astype(bf16)
    down_sum = lax.psum_scatter(
        jnp.dot(
            lax.slice_in_dim(hidden_act, 0, tok_rows * lax.axis_size("mp"), axis=0),
            weight_down,
            preferred_element_type=f32,
        ),
        "mp",
        scatter_dimension=0,
        tiled=True,
    )
    final_out, normed_two, scale_two = norm_rows(
        first_out + down_sum + bias_down.astype(f32), gain_two_f, shift_two.astype(f32)
    )
    activations = final_out.astype(bf16)
    grad_final = row_weight[:, None] * cotangent.astype(f32)
    grad_h2, grad_gain_two, grad_shift_two = norm_back(
        grad_final, normed_two, scale_two, gain_two_f
    )
    grad_bias_down = jnp.sum(grad_h2, axis=0)
    whole_grad_down = lax.all_gather(grad_h2.astype(bf16), "mp", axis=0, tiled=True)
    grad_weight_down = jnp.einsum(
        "rf,rd->fd", hidden_act, whole_grad_down, preferred_element_type=f32
    )
    grad_act = jnp.einsum("rd,fd->rf", whole_grad_down, weight_down, preferred_element_type=f32)
    grad_pre = gelu_pull(grad_act)[0].astype(bf16)
    grad_bias_in = jnp.sum(grad_pre.astype(f32), axis=0)
    grad_weight_in = jnp.einsum("rd,rf->df", whole_first, grad_pre, preferred_element_type=f32)
    grad_first = grad_h2 + lax.psum_scatter(
        jnp.einsum("rf,df->rd", grad_pre, weight_in, preferred_element_type=f32),
        "mp",
        scatter_dimension=0,
        tiled=True,
    )
    grad_h1, grad_gain_one, grad_shift_one = norm_back(
        grad_first, normed_one, scale_one, gain_one_f
    )
    grad_bias_out = jnp.sum(grad_h1, axis=0)
    whole_grad_attn = lax.all_gather(grad_h1.astype(bf16), "mp", axis=0, tiled=True)
    grad_weight_out = jnp.einsum("rc,rd->cd", context, whole_grad_attn, preferred_element_type=f32)
    grad_context = (
        jnp.einsum("rd,cd->rc", whole_grad_attn, weight_out, preferred_element_type=f32)
        .astype(bf16)
        .reshape(block_shape)
    )

    def attend_back(block_items):
        q_blk, k_blk, v_blk, len_blk, log_blk, dctx_blk = block_items
        scores = block_scores(q_blk, k_blk, len_blk)
        attn_probs = jnp.exp(scores - log_blk[..., None])
        grad_probs = jnp.einsum("sqhe,skhe->shqk", dctx_blk, v_blk, preferred_element_type=f32)
        grad_value = jnp.einsum(
            "shqk,sqhe->skhe", attn_probs.astype(bf16), dctx_blk, preferred_element_type=f32
        ).astype(bf16)
        grad_scores = (
            attn_probs * (grad_probs - jnp.sum(grad_probs * attn_probs, axis=-1, keepdims=True))
        ).astype(bf16)
        grad_query = (
            jnp.einsum("shqk,skhe->sqhe", grad_scores, k_blk, preferred_element_type=f32) * 0.125
        ).astype(bf16)
        grad_key = (
            jnp.einsum("shqk,sqhe->skhe", grad_scores, q_blk, preferred_element_type=f32) * 0.125
        ).astype(bf16)
        return jnp.stack([grad_query, grad_key, grad_value], axis=3)

    grad_mixed = lax.map(
        attend_back, (queries, key_rows, value_rows, len_blocks, log_totals, grad_context)
    )
    grad_mixed = grad_mixed.reshape(rows_all, head_count * 3 * HD)
    grad_weight_qkv = jnp.einsum("rd,rc->dc", whole_in, grad_mixed, preferred_element_type=f32)
    grad_parts = jnp.sum(grad_mixed.astype(f32).reshape(rows_all, head_count, 3, HD), axis=0)
    grad_bias_query = grad_parts[:, 0, :].reshape(head_count * HD)
    grad_bias_value = grad_parts[:, 2, :].reshape(head_count * HD)
    grad_embed = grad_h1 + lax.psum_scatter(
        jnp.einsum("rc,dc->rd", grad_mixed, weight_qkv, preferred_element_type=f32).astype(
            jnp.bfloat16
        ),
        "mp",
        scatter_dimension=0,
        tiled=True,
    ).astype(jnp.float32)
    (
        count_all,
        sum_gain_one,
        sum_shift_one,
        sum_bias_out,
        sum_gain_two,
        sum_shift_two,
        sum_bias_down,
    ) = lax.psum(
        (
            count_local,
            grad_gain_one,
            grad_shift_one,
            grad_bias_out,
            grad_gain_two,
            grad_shift_two,
            grad_bias_down,
        ),
        ("dp", "mp"),
    )
    factor = lax.rsqrt(count_all)
    sum_qkv, sum_query, sum_value, sum_out, sum_in, sum_bias_in, sum_down = (
        lax.psum(grad_weight_qkv.astype(jnp.bfloat16), "dp").astype(jnp.float32),
        lax.psum(grad_bias_query.astype(jnp.bfloat16), "dp").astype(jnp.float32),
        lax.psum(grad_bias_value.astype(jnp.bfloat16), "dp").astype(jnp.float32),
        lax.psum(grad_weight_out.astype(jnp.bfloat16), "dp").astype(jnp.float32),
        lax.psum(grad_weight_in.astype(jnp.bfloat16), "dp").astype(jnp.float32),
        lax.psum(grad_bias_in.astype(jnp.bfloat16), "dp").astype(jnp.float32),
        lax.psum(grad_weight_down.astype(jnp.bfloat16), "dp").astype(jnp.float32),
    )
    outgoing = (
        jnp.zeros((devices * capacity, model_width), f32)
        .at[slot_place]
        .set(grad_embed)
        .reshape(devices, capacity, model_width)
    )
    incoming = lax.all_to_all(
        outgoing.astype(jnp.bfloat16), ("dp", "mp"), split_axis=0, concat_axis=0, tiled=True
    ).astype(outgoing.dtype)
    received = jnp.where(slot_live[..., None], incoming, f32(0.0)).reshape(
        devices * capacity, model_width
    )
    grad_table = jnp.zeros(table.shape, f32).at[wanted_rows.reshape(-1)].add(received) * factor
    return (
        activations,
        grad_table,
        sum_qkv * factor,
        sum_query * factor,
        sum_value * factor,
        sum_out * factor,
        sum_bias_out * factor,
        sum_gain_one * factor,
        sum_shift_one * factor,
        sum_in * factor,
        sum_bias_in * factor,
        sum_down * factor,
        sum_bias_down * factor,
        sum_gain_two * factor,
        sum_shift_two * factor,
    )


def solution(mesh):
    placed = (
        P(("dp", "mp"), None),
        P(("dp", "mp")),
        P(("dp", "mp")),
        P(),
        P(("dp", "mp"), None),
        P(None, "mp"),
        P("mp"),
        P("mp"),
        P("mp", None),
        P(),
        P(),
        P(),
        P(None, "mp"),
        P("mp"),
        P("mp", None),
        P(),
        P(),
        P(),
        P(("dp", "mp"), None),
    )
    return jax.shard_map(
        on_device,
        mesh=mesh,
        in_specs=placed,
        out_specs=(
            P(("dp", "mp"), None),
            P(("dp", "mp"), None),
            P(None, "mp"),
            P("mp"),
            P("mp"),
            P("mp", None),
            P(),
            P(),
            P(),
            P(None, "mp"),
            P("mp"),
            P("mp", None),
            P(),
            P(),
            P(),
        ),
        check_vma=False,
    )
```

profile of v0, /device:TPU:0, one launch (start us, length us, event | category | flops | bytes accessed | tf_op | source)
XLA Modules:
  0.0 689.7 jit_solution(15730359723597608846)
XLA Ops:
  11.9 14.3 %all_to_all.19 = s32[32,1,16]{2,1,0:T(1,128)S(1)} all-to-all(s32[32,1,16]{2,1,0:T(1,128)S(1)} %bitcast.198), channel_id=1, replica_groups=mesh['dp'=8,'mp'=4] {'dp','mp'}, dimensions={0} | all-to-all | bytes 4096 | tf_op jit(solution)/shard_map/all_to_all | solution.py:63
  26.5 14.0 %gather_fusion = bf16[512,768]{1,0:T(8,128)(2,1)} fusion(bf16[15664,768]{1,0:T(8,128)(2,1)} %param.27, s32[1024]{0:T(1024)S(1)} %pad_clamp_fusion.1), kind=kCustom, calls=%fused_computation | custom fusion | bytes 1574912 | tf_op jit(solution)/shard_map/gather | solution.py:69
  43.4 19.4 %all-to-all-done.1 = bf16[32,16,768]{2,1,0:T(8,128)(2,1)S(1)} async-done(((bf16[32,16,768]{2,1,0:T(8,128)(2,1)}), bf16[32,16,768]{2,1,0:T(8,128)(2,1)S(1)}, u32[]{:S(2)}, u32[]{:S(2)}) %all-to-all-start.1) | async-done | bytes 786464 | tf_op jit(solution)/shard_map/all_to_all | solution.py:68
  67.4 11.9 %all-reduce = bf16[16]{0:T(256)(128)(2,1)S(1)} all-reduce(bf16[16]{0:T(256)(128)(2,1)S(1)} %dynamic-update-slice), channel_id=1, replica_groups=mesh['dp'=8,'mp'=4] {'mp'}, use_global_device_ids=true, to_apply=%add | all-reduce | flops 16 | bytes 64
  80.2 21.7 %all-gather.12.cloned.1.call-done = bf16[1024,768]{1,0:T(8,128)(2,1)} async-done(((bf16[256,768]{1,0:T(8,128)(2,1)}), bf16[1024,768]{1,0:T(8,128)(2,1)}) %all-gather.12.cloned.1.call-update) | async-done | bytes 1572880 | tf_op jit(solution)/shard_map/all_gather | solution.py:87
  115.4 4.8 while.24
  128.3 57.3 %reduce-scatter.5.cloned.1.call-done = f32[256,768]{1,0:T(8,128)} async-done(((f32[1024,768]{1,0:T(8,128)}), f32[256,768]{1,0:T(8,128)}) %reduce-scatter.5.cloned.1.call-update) | async-done | bytes 786448 | tf_op jit(solution)/shard_map/reduce_scatter | solution.py:131
  191.0 35.6 %all-gather.6.cloned.1.call-done = bf16[1024,768]{1,0:T(8,128)(2,1)} async-done(((bf16[256,768]{1,0:T(8,128)(2,1)}), bf16[1024,768]{1,0:T(8,128)(2,1)}) %all-gather.6.cloned.1.call-update) | async-done | bytes 1572880 | tf_op jit(solution)/shard_map/all_gather | solution.py:142
  226.6 10.6 %multiply_convert_fusion.1 = (bf16[1024,768]{1,0:T(8,128)(2,1)S(1)}, f32[1024,768]{1,0:T(8,128)}, f32[1024,768]{1,0:T(8,128)}) fusion(f32[768]{0:T(1024)} %convert_element_type.189, bf16[1024,768]{1,0:T(8,128)(2,1)} %all-gather.6.cloned.1.call-done, bf16[768,768]{1,0:T(8,128)(2,1)S(1)} %copy-done), kind=kOutput, calls=%fused_computation.71 | convolution fusion | flops 1259864064 | bytes 10619904 | tf_op jit(solution)/shard_map/dot_general | solution.py:143
  254.6 46.3 %reduce-scatter.7.cloned.1.call-done = f32[256,768]{1,0:T(8,128)} async-done(((f32[1024,768]{1,0:T(8,128)}), f32[256,768]{1,0:T(8,128)}) %reduce-scatter.7.cloned.1.call-update) | async-done | bytes 786448 | tf_op jit(solution)/shard_map/reduce_scatter | solution.py:146
  307.2 37.0 %all-gather.8.cloned.1.call-done = bf16[1024,768]{1,0:T(8,128)(2,1)} async-done(((bf16[256,768]{1,0:T(8,128)(2,1)}), bf16[1024,768]{1,0:T(8,128)(2,1)}) %all-gather.8.cloned.1.call-update) | async-done | bytes 1572880 | tf_op jit(solution)/shard_map/all_gather | solution.py:165
  344.3 6.4 fusion.61
  355.0 59.4 %reduce-scatter.9.cloned.1.call-done = f32[256,768]{1,0:T(8,128)} async-done(((f32[1024,768]{1,0:T(8,128)}), f32[256,768]{1,0:T(8,128)}) %reduce-scatter.9.cloned.1.call-update) | async-done | bytes 786448 | tf_op jit(solution)/shard_map/reduce_scatter | solution.py:173
  418.8 36.6 %all-gather.10.cloned.1.call-done = bf16[1024,768]{1,0:T(8,128)(2,1)} async-done(((bf16[256,768]{1,0:T(8,128)(2,1)}), bf16[1024,768]{1,0:T(8,128)(2,1)}) %all-gather.10.cloned.1.call-update) | async-done | bytes 1572880 | tf_op jit(solution)/shard_map/all_gather | solution.py:183
  458.0 16.8 %while.25 = (s32[]{:T(128)}, bf16[2,8,64,3,3,64]{5,2,3,1,4,0:T(8,128)(2,1)}, bf16[2,8,64,3,64]{4,2,3,1,0:T(8,128)(2,1)S(1)}, f32[2,8]{1,0:T(2,128)S(1)}, bf16[2,...) while((s32[]{:T(128)}, ...), condition=%wide.region_23.24_spmd.clone, body=%wide.region_21.23_spmd.clone.sunk | while | flops 66059264 | bytes 22653772 | solution.py:210
  474.8 3.5 copy.153
  481.0 4.2 convolution_convert_fusion.2
  486.0 4.0 convolution_convert_fusion.3
  492.6 41.3 %all-reduce.1 = (f32[]{:T(128)}, f32[768]{0:T(1024)S(1)}, f32[768]{0:T(1024)S(1)}, f32[768]{0:T(1024)S(1)}, f32[768]{0:T(1024)S(1)}, /*index=5*/f32[768]{0:T(1024)S(1)}, f32[768]{0:T(1024)S(1)}) all-reduce(f32[]{:T(128)S(6)} %convert_element_type.207, f32[768]{0:T(1024)S(1)} %copy-done.29, ...), channel_id=1, replica_groups=mesh['dp'=8,'mp'=4] {'dp','mp'}, use_global_device_ids=true, to_apply=%region_28.29 | all-reduce | flops 4609 | bytes 36872 | tf_op jit(solution)/shard_map/psum | solution.py:234
  537.0 3.8 convolution_convert_fusion.5
  544.0 13.8 %all-reduce.2 = (bf16[192]{0:T(256)(128)(2,1)S(1)}, bf16[192]{0:T(256)(128)(2,1)S(1)}, bf16[768]{0:T(1024)(128)(2,1)S(1)}) all-reduce(bf16[192]{0:T(256)(128)(2,1)S(1)} %convert_element_type.211, bf16[192]{0:T(256)(128)(2,1)S(1)} %convert_element_type.213, bf16[768]{0:T(1024)(128)(2,1)S(1)} %copy-done.35), channel_id=1, replica_groups=mesh['dp'=8,'mp'=4] {'dp'}, use_global_device_ids=true, to_apply=%region_31.32 | all-reduce | flops 1152 | bytes 4608 | tf_op jit(solution)/shard_map/psum | solution.py:249
  565.9 52.4 %all-reduce.6.cloned.1.call-done = (bf16[768,576]{0,1:T(8,128)(2,1)}, bf16[192,768]{1,0:T(8,128)(2,1)}, bf16[768,768]{1,0:T(8,128)(2,1)}, bf16[768,768]{1,0:T(8,128)(2,1)}) async-done(((bf16[768,576]{0,1:T(8,128)(2,1)}, bf16[192,768]{1,0:T(8,128)(2,1)}, bf16[768,768]{1,0:T(8,128)(2,1)}, bf16[768,768]{1,0:T(8,128)(2,1)}), (bf16[768,576]{0,1:T(8,128)(2,1)}, bf16[192,768]{1,0:T(8,128)(2,1)}, ...) | async-done | bytes 3538960 | tf_op jit(solution)/shard_map/psum | solution.py:248
  626.1 23.7 %scatter_custom_fusion.2 = f32[15664,768]{1,0:T(8,128)} fusion(s32[512]{0:T(512)} %copy-done.32, f32[512,768]{1,0:T(8,128)S(1)} %bitcast.197, f32[]{:T(128)} %constant.48.clone.1), kind=kCustom, calls=%fused_computation.66 | custom fusion | flops 393216 | bytes 48120320 | tf_op jit(solution)/shard_map/scatter-add | solution.py:268
  649.8 33.1 %broadcast_multiply_fusion = f32[15664,768]{1,0:T(8,128)} fusion(f32[15664,768]{1,0:T(8,128)} %scatter_custom_fusion.2, f32[]{:T(128)S(6)} %rsqrt.21), kind=kLoop, calls=%fused_computation.65 | loop fusion | flops 12029952 | bytes 96239616 | tf_op jit(solution)/shard_map/mul | solution.py:268
  (278 shorter events, 122.4 us)
Async XLA Ops:
  7.2 219.4 %copy-start = (bf16[768,768]{1,0:T(8,128)(2,1)S(1)}, bf16[768,768]{1,0:T(8,128)(2,1)}, u32[]{:S(2)}) copy-start(bf16[768,768]{1,0:T(8,128)(2,1)} %param.35) | copy-start | bytes 3538948
  10.2 33.1 %copy-start.33 = (s32[256,1]{0,1:T(1,128)}, s32[256,1]{0,1:T(1,128)S(1)}, u32[]{:S(2)}) copy-start(s32[256,1]{0,1:T(1,128)S(1)} %compare_select_fusion) | copy-start | bytes 3076
  40.5 24.3 %copy-start.44 = (u32[32]{0:T(128)S(1)}, u32[32]{0:T(128)}, u32[]{:S(2)}) copy-start(u32[32]{0:T(128)} %constant.171) | copy-start | bytes 388
  40.5 25.6 %copy-start.38 = (s32[4]{0:T(128)S(1)}, s32[4]{0:T(128)}, u32[]{:S(2)}) copy-start(s32[4]{0:T(128)} %param.25) | copy-start | bytes 52
  40.5 39.5 %copy-start.36 = (bf16[192]{0:T(256)(128)(2,1)S(1)}, bf16[192]{0:T(256)(128)(2,1)}, u32[]{:S(2)}) copy-start(bf16[192]{0:T(256)(128)(2,1)} %param.29) | copy-start | bytes 1156
  40.5 39.6 %copy-start.37 = (bf16[192]{0:T(256)(128)(2,1)S(1)}, bf16[192]{0:T(256)(128)(2,1)}, u32[]{:S(2)}) copy-start(bf16[192]{0:T(256)(128)(2,1)} %param.30) | copy-start | bytes 1156
  40.5 22.3 %all-to-all-start.1 = ((bf16[32,16,768]{2,1,0:T(8,128)(2,1)}), bf16[32,16,768]{2,1,0:T(8,128)(2,1)S(1)}, u32[]{:S(2)}, u32[]{:S(2)}) async-start(bf16[32,16,768]{2,1,0:T(8,128)(2,1)} %bitcast.6), calls=%async_computation.1 | async-start | bytes 1572864 | tf_op jit(solution)/shard_map/all_to_all | solution.py:68
  43.3 58.5 %all-gather.12.cloned.1.call-start = ((), (), s32[]{:S(2)}) async-start(), calls=%async_computation.14 | async-start | bytes 1966080 | tf_op jit(solution)/shard_map/all_gather | solution.py:87
  64.7 120.9 %reduce-scatter.5.cloned.1.call-start = ((), (), s32[]{:S(2)}) async-start(), calls=%async_computation.7 | async-start | bytes 3932160 | tf_op jit(solution)/shard_map/reduce_scatter | solution.py:131
  126.3 100.3 %all-gather.6.cloned.1.call-start = ((), (), s32[]{:S(2)}) async-start(), calls=%async_computation.8 | async-start | bytes 1966080 | tf_op jit(solution)/shard_map/all_gather | solution.py:142
  189.5 111.4 %reduce-scatter.7.cloned.1.call-start = ((), (), s32[]{:S(2)}) async-start(), calls=%async_computation.9 | async-start | bytes 3932160 | tf_op jit(solution)/shard_map/reduce_scatter | solution.py:146
  241.5 102.7 %all-gather.8.cloned.1.call-start = ((), (), s32[]{:S(2)}) async-start(), calls=%async_computation.10 | async-start | bytes 1966080 | tf_op jit(solution)/shard_map/all_gather | solution.py:165
  307.2 107.2 %reduce-scatter.9.cloned.1.call-start = ((), (), s32[]{:S(2)}) async-start(), calls=%async_computation.11 | async-start | bytes 3932160 | tf_op jit(solution)/shard_map/reduce_scatter | solution.py:173
  354.9 59.5 %copy-start.11 = (f32[256,768]{1,0:T(8,128)S(1)}, f32[256,768]{1,0:T(8,128)}, u32[]{:S(2)}) copy-start(f32[256,768]{1,0:T(8,128)} %copy-done.10) | copy-start | bytes 2359300
  354.9 59.5 %copy-start.23 = (f32[256]{0:T(256)S(1)}, f32[256]{0:T(256)}, u32[]{:S(2)}) copy-start(f32[256]{0:T(256)} %copy-done.22) | copy-start | bytes 3076
  354.9 100.5 %all-gather.10.cloned.1.call-start = ((), (), s32[]{:S(2)}) async-start(), calls=%async_computation.12 | async-start | bytes 1966080 | tf_op jit(solution)/shard_map/all_gather | solution.py:183
  417.4 38.0 %copy-start.8 = (f32[256,768]{1,0:T(8,128)}, f32[256,768]{1,0:T(8,128)S(1)}, u32[]{:S(2)}) copy-start(f32[256,768]{1,0:T(8,128)S(1)} %get-tuple-element.276) | copy-start | bytes 2359300
  417.4 40.6 %copy-start.43 = (f32[2,8]{1,0:T(2,128)S(1)}, f32[2,8]{1,0:T(2,128)}, u32[]{:S(2)}) copy-start(f32[2,8]{1,0:T(2,128)} %reshape.323) | copy-start | bytes 196
  418.3 140.0 %reduce-scatter.11.cloned.1.call-start = ((), (), s32[]{:S(2)}) async-start(), calls=%async_computation.13 | async-start | bytes 1966080 | tf_op jit(solution)/shard_map/reduce_scatter | solution.py:218
  485.2 133.0 %all-reduce.6.cloned.1.call-start = ((), (), s32[]{:S(2)}) async-start(), calls=%async_computation.15 | async-start | bytes 7077888 | tf_op jit(solution)/shard_map/psum | solution.py:248
  490.1 45.7 %copy-start.12 = (bf16[1024,192]{0,1:T(8,128)(2,1)S(1)}, bf16[1024,192]{0,1:T(8,128)(2,1)}, u32[]{:S(2)}) copy-start(bf16[1024,192]{0,1:T(8,128)(2,1)} %reshape.315) | copy-start | bytes 1179652
  490.1 45.7 %copy-start.13 = (bf16[1024,768]{1,0:T(8,128)(2,1)S(1)}, bf16[1024,768]{1,0:T(8,128)(2,1)}, u32[]{:S(2)}) copy-start(bf16[1024,768]{1,0:T(8,128)(2,1)} %all-gather.10.cloned.1.call-done) | copy-start | bytes 4718596
  561.6 64.2 %all-to-all-start.2 = ((bf16[32,16,768]{2,1,0:T(8,128)(2,1)}), bf16[32,16,768]{2,1,0:T(8,128)(2,1)S(1)}, u32[]{:S(2)}, u32[]{:S(2)}) async-start(bf16[32,16,768]{2,1,0:T(8,128)(2,1)} %bitcast.12), calls=%async_computation.6 | async-start | bytes 1572864 | tf_op jit(solution)/shard_map/all_to_all | solution.py:262
  649.8 33.1 %copy-start.1 = (bf16[768,768]{1,0:T(8,128)(2,1)S(1)}, bf16[768,768]{1,0:T(8,128)(2,1)}, u32[]{:S(2)}) copy-start(bf16[768,768]{1,0:T(8,128)(2,1)} %param.35) | copy-start | bytes 3538948
  (43 other events, 135.5 us)
Sparse Core Ops, SparseCore 0:
  64.8 36.9 all-gather.11
  126.4 59.2 reduce-scatter.4
  189.6 36.9 all-gather.5
  241.6 59.2 reduce-scatter.6
  307.3 36.9 all-gather.7
  355.1 59.2 reduce-scatter.8
  418.4 36.9 all-gather.9
  485.3 35.0 reduce-scatter.10
  540.9 77.2 all-reduce.5
where the time goes:
time: 697 us; the launch traced here: 690 us
  waiting for transfers between devices  366 us (53%)
  other arithmetic  109 us (16%)
  blocking collectives  81.4 us (12%)
  local copies, waits for them, and re-layouts  58.3 us (8%)
  matrix products  51.5 us (7%)
  between operations  16.5 us (2%)
    reduce_scatter x1, waiting for transfers between devices, on_device(): lax.psum_scatter(jnp.einsum('rf,df->rd', grad_pre, weight_in, preferred_e...  59.4 us
    reduce_scatter x1, waiting for transfers between devices, on_device(): lax.psum_scatter(jnp.dot(context, weight_out, preferred_element_type=f32)...  57.3 us
    psum x1, waiting for transfers between devices, on_device(): lax.psum(grad_weight_qkv.astype(jnp.bfloat16), 'dp').astype(jnp.float32)  52.4 us
    reduce_scatter x1, waiting for transfers between devices, on_device(): lax.psum_scatter(jnp.dot(lax.slice_in_dim(hidden_act, 0, tok_rows * lax.a...  46.3 us
    psum x1, blocking collectives, on_device(): lax.psum((count_local, grad_gain_one, grad_shift_one, grad_bias_out, grad...  41.3 us
    all_gather x1, waiting for transfers between devices, on_device(): lax.all_gather(grad_h2.astype(bf16), 'mp', axis=0, tiled=True)  37 us
    all_gather x1, waiting for transfers between devices, on_device(): lax.all_gather(grad_h1.astype(bf16), 'mp', axis=0, tiled=True)  36.6 us
    all_gather x1, waiting for transfers between devices, on_device(): lax.all_gather(first_out.astype(bf16), 'mp', axis=0, tiled=True)  35.6 us
  transfers between devices with their start and end apart: 11, of which 9 were waited for; matrix products, arithmetic and copies ran while one was open for 7% of the time, Pallas kernels for 0%

commit v1 on v0

--- a/solution.py
+++ b/solution.py
@@ -162,7 +162,9 @@
         grad_final, normed_two, scale_two, gain_two_f
     )
     grad_bias_down = jnp.sum(grad_h2, axis=0)
-    whole_grad_down = lax.all_gather(grad_h2.astype(bf16), "mp", axis=0, tiled=True)
+    whole_grad_down = jnp.concatenate(
+        lax.all_to_all(jnp.stack([grad_h2.astype(bf16)] * lax.axis_size("mp")), "mp", 0, 0), axis=0
+    )
     grad_weight_down = jnp.einsum(
         "rf,rd->fd", hidden_act, whole_grad_down, preferred_element_type=f32
     )

time: 697 us -> 699 us (level)
  blocking collectives: 81.4 us -> 122 us
  waiting for transfers between devices: 366 us -> 329 us
    all_to_all x0 -> x1, blocking collectives: none -> 40.6 us  [on_device(): lax.all_to_all(jnp.stack([grad_h2.astype(bf16)] * lax.axis_size('mp')), '...]
    all_gather x1 -> x0, waiting for transfers between devices: 37 us -> none  [on_device(): lax.all_gather(grad_h2.astype(bf16), 'mp', axis=0, tiled=True)]
  transfers between devices with their start and end apart: 11 -> 10, of which waited for: 9 -> 8; matrix products, arithmetic and copies ran while one was open for 7% -> 7% of each run, Pallas kernels for 0% -> 0%
where the time goes in v1:
time: 699 us; the launch traced here: 691 us
  waiting for transfers between devices  329 us (47%)
  blocking collectives  122 us (17%)
  other arithmetic  109 us (16%)
  local copies, waits for them, and re-layouts  60.4 us (9%)
  matrix products  46.9 us (7%)
  between operations  16.9 us (2%)
    reduce_scatter x1, waiting for transfers between devices, on_device(): lax.psum_scatter(jnp.einsum('rf,df->rd', grad_pre, weight_in, preferred_e...  59.5 us
    reduce_scatter x1, waiting for transfers between devices, on_device(): lax.psum_scatter(jnp.dot(context, weight_out, preferred_element_type=f32)...  57.3 us
    psum x1, waiting for transfers between devices, on_device(): lax.psum(grad_weight_qkv.astype(jnp.bfloat16), 'dp').astype(jnp.float32)  52.3 us
    reduce_scatter x1, waiting for transfers between devices, on_device(): lax.psum_scatter(jnp.dot(lax.slice_in_dim(hidden_act, 0, tok_rows * lax.a...  46.3 us
    psum x1, blocking collectives, on_device(): lax.psum((count_local, grad_gain_one, grad_shift_one, grad_bias_out, grad...  41.3 us
    all_to_all x1, blocking collectives, on_device(): lax.all_to_all(jnp.stack([grad_h2.astype(bf16)] * lax.axis_size('mp')), '...  40.6 us
    all_gather x1, waiting for transfers between devices, on_device(): lax.all_gather(grad_h1.astype(bf16), 'mp', axis=0, tiled=True)  36.6 us
    all_gather x1, waiting for transfers between devices, on_device(): lax.all_gather(first_out.astype(bf16), 'mp', axis=0, tiled=True)  35.5 us
  transfers between devices with their start and end apart: 10, of which 8 were waited for; matrix products, arithmetic and copies ran while one was open for 7% of the time, Pallas kernels for 0%

profile of v1, /device:TPU:0, one launch (start us, length us, event | category | flops | bytes accessed | tf_op | source)
XLA Modules:
  0.0 691.3 jit_solution(10659765033091142563)
XLA Ops:
  11.9 14.3 %all_to_all.24 = s32[32,1,16]{2,1,0:T(1,128)S(1)} all-to-all(s32[32,1,16]{2,1,0:T(1,128)S(1)} %bitcast.201), channel_id=1, replica_groups=mesh['dp'=8,'mp'=4] {'dp','mp'}, dimensions={0} | all-to-all | bytes 4096 | tf_op jit(solution)/shard_map/all_to_all | solution.py:63
  26.5 14.0 %gather_fusion = bf16[512,768]{1,0:T(8,128)(2,1)} fusion(bf16[15664,768]{1,0:T(8,128)(2,1)} %param.27, s32[1024]{0:T(1024)S(1)} %pad_clamp_fusion.1), kind=kCustom, calls=%fused_computation | custom fusion | bytes 1574912 | tf_op jit(solution)/shard_map/gather | solution.py:69
  43.4 19.4 %all-to-all-done.1 = bf16[32,16,768]{2,1,0:T(8,128)(2,1)S(1)} async-done(((bf16[32,16,768]{2,1,0:T(8,128)(2,1)}), bf16[32,16,768]{2,1,0:T(8,128)(2,1)S(1)}, u32[]{:S(2)}, u32[]{:S(2)}) %all-to-all-start.1) | async-done | bytes 786464 | tf_op jit(solution)/shard_map/all_to_all | solution.py:68
  67.4 12.0 %all-reduce = bf16[16]{0:T(256)(128)(2,1)S(1)} all-reduce(bf16[16]{0:T(256)(128)(2,1)S(1)} %dynamic-update-slice), channel_id=1, replica_groups=mesh['dp'=8,'mp'=4] {'mp'}, use_global_device_ids=true, to_apply=%add | all-reduce | flops 16 | bytes 64
  80.2 21.7 %all-gather.9.cloned.1.call-done = bf16[1024,768]{1,0:T(8,128)(2,1)} async-done(((bf16[256,768]{1,0:T(8,128)(2,1)}), bf16[1024,768]{1,0:T(8,128)(2,1)}) %all-gather.9.cloned.1.call-update) | async-done | bytes 1572880 | tf_op jit(solution)/shard_map/all_gather | solution.py:87
  114.7 4.8 while.24
  127.6 57.3 %reduce-scatter.5.cloned.1.call-done = f32[256,768]{1,0:T(8,128)} async-done(((f32[1024,768]{1,0:T(8,128)}), f32[256,768]{1,0:T(8,128)}) %reduce-scatter.5.cloned.1.call-update) | async-done | bytes 786448 | tf_op jit(solution)/shard_map/reduce_scatter | solution.py:131
  190.3 35.5 %all-gather.5.cloned.1.call-done = bf16[1024,768]{1,0:T(8,128)(2,1)} async-done(((bf16[256,768]{1,0:T(8,128)(2,1)}), bf16[1024,768]{1,0:T(8,128)(2,1)}) %all-gather.5.cloned.1.call-update) | async-done | bytes 1572880 | tf_op jit(solution)/shard_map/all_gather | solution.py:142
  225.9 10.6 %multiply_convert_fusion.1 = (bf16[1024,768]{1,0:T(8,128)(2,1)S(1)}, f32[1024,768]{1,0:T(8,128)}, f32[1024,768]{1,0:T(8,128)}) fusion(f32[768]{0:T(1024)} %convert_element_type.189, bf16[1024,768]{1,0:T(8,128)(2,1)} %all-gather.5.cloned.1.call-done, bf16[768,768]{1,0:T(8,128)(2,1)S(1)} %copy-done), kind=kOutput, calls=%fused_computation.71 | convolution fusion | flops 1259864064 | bytes 10619904 | tf_op jit(solution)/shard_map/dot_general | solution.py:143
  253.9 46.3 %reduce-scatter.7.cloned.1.call-done = f32[256,768]{1,0:T(8,128)} async-done(((f32[1024,768]{1,0:T(8,128)}), f32[256,768]{1,0:T(8,128)}) %reduce-scatter.7.cloned.1.call-update) | async-done | bytes 786448 | tf_op jit(solution)/shard_map/reduce_scatter | solution.py:146
  305.8 40.6 %all_to_all.25 = bf16[4,256,768]{2,1,0:T(8,128)(2,1)S(1)} all-to-all(bf16[4,256,768]{2,1,0:T(8,128)(2,1)S(1)} %stack.19), channel_id=1, replica_groups=mesh['dp'=8,'mp'=4] {'mp'}, dimensions={0} | all-to-all | bytes 3145728 | tf_op jit(solution)/shard_map/all_to_all | solution.py:166
  353.6 59.5 %reduce-scatter.9.cloned.1.call-done = f32[256,768]{1,0:T(8,128)} async-done(((f32[1024,768]{1,0:T(8,128)}), f32[256,768]{1,0:T(8,128)}) %reduce-scatter.9.cloned.1.call-update) | async-done | bytes 786448 | tf_op jit(solution)/shard_map/reduce_scatter | solution.py:175
  417.5 36.6 %all-gather.7.cloned.1.call-done = bf16[1024,768]{1,0:T(8,128)(2,1)} async-done(((bf16[256,768]{1,0:T(8,128)(2,1)}), bf16[1024,768]{1,0:T(8,128)(2,1)}) %all-gather.7.cloned.1.call-update) | async-done | bytes 1572880 | tf_op jit(solution)/shard_map/all_gather | solution.py:185
  456.8 16.8 %while.25 = (s32[]{:T(128)}, bf16[2,8,64,3,3,64]{5,2,3,1,4,0:T(8,128)(2,1)}, bf16[2,8,64,3,64]{4,2,3,1,0:T(8,128)(2,1)S(1)}, f32[2,8]{1,0:T(2,128)S(1)}, bf16[2,...) while((s32[]{:T(128)}, ...), condition=%wide.region_23.24_spmd.clone, body=%wide.region_21.23_spmd.clone.sunk | while | flops 66059264 | bytes 22653772 | solution.py:212
  473.6 4.6 copy.153
  478.1 3.5 reshape.325
  481.6 3.9 convolution_convert_fusion.2
  486.3 4.0 convolution_convert_fusion.3
  492.9 41.3 %all-reduce.1 = (f32[]{:T(128)}, f32[768]{0:T(1024)S(1)}, f32[768]{0:T(1024)S(1)}, f32[768]{0:T(1024)S(1)}, f32[768]{0:T(1024)S(1)}, /*index=5*/f32[768]{0:T(1024)S(1)}, f32[768]{0:T(1024)S(1)}) all-reduce(f32[]{:T(128)S(6)} %convert_element_type.207, f32[768]{0:T(1024)S(1)} %copy-done.30, ...), channel_id=1, replica_groups=mesh['dp'=8,'mp'=4] {'dp','mp'}, use_global_device_ids=true, to_apply=%region_28.29 | all-reduce | flops 4609 | bytes 36872 | tf_op jit(solution)/shard_map/psum | solution.py:236
  537.3 3.4 convolution_convert_fusion.5
  545.5 13.9 %all-reduce.2 = (bf16[192]{0:T(256)(128)(2,1)S(1)}, bf16[192]{0:T(256)(128)(2,1)S(1)}, bf16[768]{0:T(1024)(128)(2,1)S(1)}) all-reduce(bf16[192]{0:T(256)(128)(2,1)S(1)} %convert_element_type.211, bf16[192]{0:T(256)(128)(2,1)S(1)} %convert_element_type.213, bf16[768]{0:T(1024)(128)(2,1)S(1)} %copy-done.37), channel_id=1, replica_groups=mesh['dp'=8,'mp'=4] {'dp'}, use_global_device_ids=true, to_apply=%region_31.32 | all-reduce | flops 1152 | bytes 4608 | tf_op jit(solution)/shard_map/psum | solution.py:251
  567.3 52.3 %all-reduce.6.cloned.1.call-done = (bf16[768,576]{0,1:T(8,128)(2,1)}, bf16[192,768]{1,0:T(8,128)(2,1)}, bf16[768,768]{1,0:T(8,128)(2,1)}, bf16[768,768]{1,0:T(8,128)(2,1)}) async-done(((bf16[768,576]{0,1:T(8,128)(2,1)}, bf16[192,768]{1,0:T(8,128)(2,1)}, bf16[768,768]{1,0:T(8,128)(2,1)}, bf16[768,768]{1,0:T(8,128)(2,1)}), (bf16[768,576]{0,1:T(8,128)(2,1)}, bf16[192,768]{1,0:T(8,128)(2,1)}, ...) | async-done | bytes 3538960 | tf_op jit(solution)/shard_map/psum | solution.py:250
  627.5 23.7 %scatter_custom_fusion.2 = f32[15664,768]{1,0:T(8,128)} fusion(s32[512]{0:T(512)} %copy-done.33, f32[512,768]{1,0:T(8,128)S(1)} %bitcast.200, f32[]{:T(128)} %constant.48.clone.1), kind=kCustom, calls=%fused_computation.66 | custom fusion | flops 393216 | bytes 48120320 | tf_op jit(solution)/shard_map/scatter-add | solution.py:270
  651.2 33.1 %broadcast_multiply_fusion = f32[15664,768]{1,0:T(8,128)} fusion(f32[15664,768]{1,0:T(8,128)} %scatter_custom_fusion.2, f32[]{:T(128)S(6)} %rsqrt.21), kind=kLoop, calls=%fused_computation.65 | loop fusion | flops 12029952 | bytes 96239616 | tf_op jit(solution)/shard_map/mul | solution.py:270
  (287 shorter events, 122.6 us)
Async XLA Ops:
  7.2 218.7 %copy-start = (bf16[768,768]{1,0:T(8,128)(2,1)S(1)}, bf16[768,768]{1,0:T(8,128)(2,1)}, u32[]{:S(2)}) copy-start(bf16[768,768]{1,0:T(8,128)(2,1)} %param.35) | copy-start | bytes 3538948
  40.5 39.5 %copy-start.38 = (bf16[192]{0:T(256)(128)(2,1)S(1)}, bf16[192]{0:T(256)(128)(2,1)}, u32[]{:S(2)}) copy-start(bf16[192]{0:T(256)(128)(2,1)} %param.29) | copy-start | bytes 1156
  40.5 39.6 %copy-start.39 = (bf16[192]{0:T(256)(128)(2,1)S(1)}, bf16[192]{0:T(256)(128)(2,1)}, u32[]{:S(2)}) copy-start(bf16[192]{0:T(256)(128)(2,1)} %param.30) | copy-start | bytes 1156
  40.5 61.3 %copy-start.44 = (bf16[768,576]{0,1:T(8,128)(2,1)S(1)}, bf16[768,576]{0,1:T(8,128)(2,1)}, u32[]{:S(2)}) copy-start(bf16[768,576]{0,1:T(8,128)(2,1)} %param.28) | copy-start | bytes 2654212
  40.5 22.3 %all-to-all-start.1 = ((bf16[32,16,768]{2,1,0:T(8,128)(2,1)}), bf16[32,16,768]{2,1,0:T(8,128)(2,1)S(1)}, u32[]{:S(2)}, u32[]{:S(2)}) async-start(bf16[32,16,768]{2,1,0:T(8,128)(2,1)} %bitcast.6), calls=%async_computation.1 | async-start | bytes 1572864 | tf_op jit(solution)/shard_map/all_to_all | solution.py:68
  43.3 58.5 %all-gather.9.cloned.1.call-start = ((), (), s32[]{:S(2)}) async-start(), calls=%async_computation.14 | async-start | bytes 1966080 | tf_op jit(solution)/shard_map/all_gather | solution.py:87
  64.7 120.2 %reduce-scatter.5.cloned.1.call-start = ((), (), s32[]{:S(2)}) async-start(), calls=%async_computation.8 | async-start | bytes 3932160 | tf_op jit(solution)/shard_map/reduce_scatter | solution.py:131
  125.6 100.3 %all-gather.5.cloned.1.call-start = ((), (), s32[]{:S(2)}) async-start(), calls=%async_computation.9 | async-start | bytes 1966080 | tf_op jit(solution)/shard_map/all_gather | solution.py:142
  188.8 111.4 %reduce-scatter.7.cloned.1.call-start = ((), (), s32[]{:S(2)}) async-start(), calls=%async_computation.10 | async-start | bytes 3932160 | tf_op jit(solution)/shard_map/reduce_scatter | solution.py:146
  240.8 172.3 %reduce-scatter.9.cloned.1.call-start = ((), (), s32[]{:S(2)}) async-start(), calls=%async_computation.11 | async-start | bytes 3932160 | tf_op jit(solution)/shard_map/reduce_scatter | solution.py:175
  303.0 43.4 %copy-start.52 = (f32[1024,768]{1,0:T(8,128)S(1)}, f32[1024,768]{1,0:T(8,128)}, u32[]{:S(2)}) copy-start(f32[1024,768]{1,0:T(8,128)} %get-tuple-element.298) | copy-start | bytes 9437188
  305.6 40.7 %copy-start.35 = (f32[768]{0:T(1024)S(1)}, f32[768]{0:T(1024)}, u32[]{:S(2)}) copy-start(f32[768]{0:T(1024)} %convert_element_type.189) | copy-start | bytes 9220
  305.6 40.7 %copy-start.43 = (bf16[768,768]{1,0:T(8,128)(2,1)S(1)}, bf16[768,768]{1,0:T(8,128)(2,1)}, u32[]{:S(2)}) copy-start(bf16[768,768]{1,0:T(8,128)(2,1)} %param.37) | copy-start | bytes 3538948
  305.6 40.7 %copy-start.51 = (f32[1024,768]{1,0:T(8,128)S(1)}, f32[1024,768]{1,0:T(8,128)}, u32[]{:S(2)}) copy-start(f32[1024,768]{1,0:T(8,128)} %get-tuple-element.281) | copy-start | bytes 9437188
  353.5 59.6 %copy-start.10 = (f32[256,768]{1,0:T(8,128)S(1)}, f32[256,768]{1,0:T(8,128)}, u32[]{:S(2)}) copy-start(f32[256,768]{1,0:T(8,128)} %copy-done.9) | copy-start | bytes 2359300
  353.5 59.6 %copy-start.24 = (f32[256]{0:T(256)S(1)}, f32[256]{0:T(256)}, u32[]{:S(2)}) copy-start(f32[256]{0:T(256)} %copy-done.23) | copy-start | bytes 3076
  353.5 100.6 %all-gather.7.cloned.1.call-start = ((), (), s32[]{:S(2)}) async-start(), calls=%async_computation.12 | async-start | bytes 1966080 | tf_op jit(solution)/shard_map/all_gather | solution.py:185
  416.2 38.0 %copy-start.7 = (f32[256,768]{1,0:T(8,128)}, f32[256,768]{1,0:T(8,128)S(1)}, u32[]{:S(2)}) copy-start(f32[256,768]{1,0:T(8,128)S(1)} %get-tuple-element.276) | copy-start | bytes 2359300
  416.2 40.6 %copy-start.46 = (f32[2,8]{1,0:T(2,128)S(1)}, f32[2,8]{1,0:T(2,128)}, u32[]{:S(2)}) copy-start(f32[2,8]{1,0:T(2,128)} %reshape.329) | copy-start | bytes 196
  417.1 142.9 %reduce-scatter.11.cloned.1.call-start = ((), (), s32[]{:S(2)}) async-start(), calls=%async_computation.13 | async-start | bytes 1966080 | tf_op jit(solution)/shard_map/reduce_scatter | solution.py:220
  485.5 134.1 %all-reduce.6.cloned.1.call-start = ((), (), s32[]{:S(2)}) async-start(), calls=%async_computation.15 | async-start | bytes 7077888 | tf_op jit(solution)/shard_map/psum | solution.py:250
  490.4 45.7 %copy-start.11 = (bf16[1024,192]{0,1:T(8,128)(2,1)S(1)}, bf16[1024,192]{0,1:T(8,128)(2,1)}, u32[]{:S(2)}) copy-start(bf16[1024,192]{0,1:T(8,128)(2,1)} %reshape.320) | copy-start | bytes 1179652
  490.4 45.7 %copy-start.14 = (bf16[1024,768]{1,0:T(8,128)(2,1)S(1)}, bf16[1024,768]{1,0:T(8,128)(2,1)}, u32[]{:S(2)}) copy-start(bf16[1024,768]{1,0:T(8,128)(2,1)} %all-gather.7.cloned.1.call-done) | copy-start | bytes 4718596
  563.3 63.9 %all-to-all-start.3 = ((bf16[32,16,768]{2,1,0:T(8,128)(2,1)}), bf16[32,16,768]{2,1,0:T(8,128)(2,1)S(1)}, u32[]{:S(2)}, u32[]{:S(2)}) async-start(bf16[32,16,768]{2,1,0:T(8,128)(2,1)} %bitcast.13), calls=%async_computation.7 | async-start | bytes 1572864 | tf_op jit(solution)/shard_map/all_to_all | solution.py:264
  (47 other events, 255.9 us)
Sparse Core Ops, SparseCore 0:
  64.9 36.9 all-gather.8
  125.7 59.2 reduce-scatter.4
  188.9 36.9 all-gather.4
  240.9 59.2 reduce-scatter.6
  353.6 59.4 reduce-scatter.8
  417.2 36.9 all-gather.6
  485.6 35.0 reduce-scatter.10
  540.9 78.6 all-reduce.5
